TPU v7x, 512 devices: a whole 4x8x8 slice. The times are simulated.
512 devices in a mesh: dp: 64 (over x, z_lo, y), tensor: 4 (over z_hi), section: 2 (over core).
Axes of the slice: x: 4, y: 8, z: 8 (z_hi: 4, z_lo: 2; z = z_hi * 2 + z_lo), core: 2. Of those that a mesh axis runs over, the one named last changes fastest.
Arguments:
- train_act: bfloat16 [2, 16384, 8192], P('section', ('dp', 'tensor')), may hold values from -6 to 6
- train_grad: bfloat16 [2, 16384, 28672], P('section', 'dp', 'tensor'), may hold values from -6 to 6
- val_act: bfloat16 [2, 256, 8192], P('section', 'dp'), may hold values from -6 to 6
- val_grad: bfloat16 [2, 256, 28672], P('section', 'dp', 'tensor'), may hold values from -6 to 6
Outputs:
- scores: float32 [16384], P(('dp', 'tensor', 'section'))
All inputs are finite; a program needn't handle non-finite values.
Results may differ from a plain program's by a relative error of at most 0.0003.
Values may be sent and summed in bfloat16 or wider, within the bound.
No kernel may reach another device: no remote copies, remote signals or barrier semaphores. Data moves between devices by JAX's collectives and lax.ppermute only.
A program may use at most 64 MiB of HBM per device.

v0:
```python
import math

import jax
import jax.numpy as jnp
from jax import lax
from jax.sharding import PartitionSpec as P


def gram_of(left, right):
    return lax.dot_general(
        left, right, (((1,), (1,)), ((), ())), preferred_element_type=jnp.float32
    )


def local(train_act, train_grad, val_act, val_grad):
    own_rows = train_act[0]
    grad_rows = train_grad[0]
    width = own_rows.shape[1]
    groups = lax.axis_size("tensor")
    hidden = grad_rows.shape[1] * groups
    val_total = val_act.shape[1] * lax.axis_size("dp")
    factor = 1.0 / math.sqrt(width * hidden * val_total)
    val_left = val_act[0]
    gathered = lax.all_gather(own_rows, "tensor", axis=0, tiled=True)
    act_gram = gram_of(gathered, lax.all_gather(val_left, "dp", axis=0, tiled=True))
    grad_gram = gram_of(grad_rows, lax.all_gather(val_grad[0], "dp", axis=0, tiled=True))
    folded = jnp.sum(act_gram * grad_gram, axis=1)
    return lax.psum_scatter(folded * factor, ("tensor", "section"), scatter_dimension=0, tiled=True)


def solution(mesh):
    in_specs = (
        P("section", ("dp", "tensor"), None),
        P("section", "dp", "tensor"),
        P("section", "dp", None),
        P("section", "dp", "tensor"),
    )
    out_specs = P(("dp", "tensor", "section"))
    return jax.shard_map(local, mesh=mesh, in_specs=in_specs, out_specs=out_specs, check_vma=False)
```

profile of v0, /device:TPU:1, one launch (start us, length us, event | category | flops | bytes accessed | tf_op | source)
XLA Modules:
  0.0 754.9 jit_solution(4883735737465029827)
XLA Ops:
  6.5 0.0 all-gather.7.cloned.1.call-start
  6.5 0.7 all-gather.7.cloned.1.call-update
  7.3 0.0 all-gather.9.cloned.1.call-start
  7.3 1.6 copy.7
  8.9 0.0 all-gather.9.cloned.1.call-update
  8.9 0.0 all-gather.11.cloned.1.call-start
  9.0 1.5 copy.8
  10.5 0.0 all-gather.11.cloned.1.call-update
  10.5 1.3 dynamic-slice
  12.5 86.8 %all-gather.7.cloned.1.call-done = bf16[1,256,8192]{2,1,0:T(8,128)(2,1)} async-done(((bf16[1,64,8192]{2,1,0:T(8,128)(2,1)}), bf16[1,256,8192]{2,1,0:T(8,128)(2,1)}) %all-gather.7.cloned.1.call-update) | async-done | bytes 4194320 | tf_op jit(solution)/shard_map/all_gather | solution.py:24
  99.3 277.0 %all-gather.9.cloned.1.call-done = bf16[1,256,8192]{2,0,1:T(2,128)(2,1)} async-done(((bf16[1,4,8192]{2,0,1:T(2,128)(2,1)}), bf16[1,256,8192]{2,0,1:T(2,128)(2,1)}) %all-gather.9.cloned.1.call-update) | async-done | bytes 4194320 | tf_op jit(solution)/shard_map/all_gather | solution.py:25
  376.3 9.7 %fusion = f32[256,256]{0,1:T(8,128)S(1)} fusion(bf16[1,256,8192]{2,0,1:T(2,128)(2,1)} %all-gather.9.cloned.1.call-done, bf16[1,256,8192]{2,1,0:T(8,128)(2,1)} %all-gather.7.cloned.1.call-done), kind=kOutput, calls=%fused_computation | convolution fusion | flops 1073741824 | bytes 8650752 | tf_op jit(solution)/shard_map/dot_general | solution.py:10
  386.0 299.9 %all-gather.11.cloned.1.call-done = bf16[1,256,7168]{2,0,1:T(2,128)(2,1)} async-done(((bf16[1,4,7168]{2,0,1:T(2,128)(2,1)}), bf16[1,256,7168]{2,0,1:T(2,128)(2,1)}) %all-gather.11.cloned.1.call-update) | async-done | bytes 3670032 | tf_op jit(solution)/shard_map/all_gather | solution.py:26
  685.9 5.7 fusion.13
  691.6 56.2 %all-reduce = f32[256]{0:T(256)S(1)} all-reduce(f32[256]{0:T(256)S(1)} %broadcast_multiply_fusion), channel_id=5, replica_groups=mesh['dp'=64,'tensor'=4,'section'=2] {'tensor','section'}, use_global_device_ids=true, to_apply=%region_1.0.clone | all-reduce | flops 256 | bytes 2048
  747.8 0.6 dynamic-slice.1
  (1 shorter events, 0.0 us)
Async XLA Ops:
  6.5 92.7 %all-gather.7.cloned.1.call-start = ((), (), s32[]{:S(2)}) async-start(), calls=%async_computation | async-start | bytes 5242880 | tf_op jit(solution)/shard_map/all_gather | solution.py:24
  7.3 369.1 %all-gather.9.cloned.1.call-start = ((), (), s32[]{:S(2)}) async-start(), calls=%async_computation.1 | async-start | bytes 8519680 | tf_op jit(solution)/shard_map/all_gather | solution.py:25
  8.9 677.0 %all-gather.11.cloned.1.call-start = ((), (), s32[]{:S(2)}) async-start(), calls=%async_computation.2 | async-start | bytes 7454720 | tf_op jit(solution)/shard_map/all_gather | solution.py:26
Sparse Core Ops, SparseCore 0:
  9.4 89.8 all-gather.6
  101.4 274.9 all-gather.8
  378.4 307.4 all-gather.10
where the time goes:
time: 755 us
  waiting for transfers between devices  664 us (88%)
  blocking collectives  56.2 us (7%)
  matrix products  15.3 us (2%)
  between operations  13.8 us (2%)
    all_gather x1, waiting for transfers between devices, local(): lax.all_gather(val_grad[0], 'dp', axis=0, tiled=True)  300 us
    all_gather x1, waiting for transfers between devices, local(): lax.all_gather(val_left, 'dp', axis=0, tiled=True)  277 us
    all_gather x1, waiting for transfers between devices, local(): gathered = lax.all_gather(own_rows, 'tensor', axis=0, tiled=True)  86.8 us
    unnamed x1, blocking collectives  56.2 us
    dot_general x2, matrix products, gram_of(): lax.dot_general(left, right, (((1,), (1,)), ((), ())), preferred_element_...  15.3 us
  transfers between devices with their start and end apart: 3, of which 3 were waited for; matrix products, arithmetic and copies ran while one was open for 2% of the time, Pallas kernels for 0%

commit v1 on v0

v1 whole, which is shorter than its diff:
```python
import math

import jax
import jax.numpy as jnp
from jax import lax
from jax.sharding import Mesh, PartitionSpec as P


CUTS = (0, 7, 14)


def gram_of(left, right):
    return lax.dot_general(
        left, right, (((1,), (1,)), ((), ())), preferred_element_type=jnp.float32
    )


def exchange(blocks, axes):
    return lax.all_to_all(blocks, axes, split_axis=0, concat_axis=0, tiled=True)


def shift(block, axis, by):
    n = lax.axis_size(axis)
    return lax.ppermute(block, axis, [(i, (i + by) % n) for i in range(n)])


def plane(blocks):
    pair, line = lax.axis_size("zl"), lax.axis_size("y")
    shape = blocks.shape[1:]
    blocks = jnp.broadcast_to(blocks[:, None], (pair, line) + shape)
    rows = exchange(blocks.reshape((pair * line,) + shape), ("zl", "y"))
    return rows.reshape(-1, shape[1])


def across(rows):
    moved = [shift(rows, "x", by) for by in (1, -1, 2)]
    return jnp.concatenate([rows, *moved])


def local(train_act, train_grad, val_act, val_grad):
    own, grad, val_a, val_g = train_act[0], train_grad[0], val_act[0], val_grad[0]
    groups, layers, pair = (lax.axis_size(axis) for axis in ("t", "s", "zl"))
    me = lax.axis_index("zl")
    rows, width = own.shape
    hidden = grad.shape[1] * groups
    half = width // pair
    val_total = val_a.shape[0] * lax.axis_size(("x", "zl", "y"))
    factor = 1.0 / math.sqrt(width * hidden * val_total)

    def columns(array, index):
        return lax.dynamic_slice_in_dim(array, index * half, half, 1)

    acts = plane(val_a.reshape(-1, pair, half).transpose(1, 0, 2))
    mine = columns(own, me)
    other = shift(columns(own, 1 - me), "zl", 1)
    unit = grad.shape[1] // CUTS[-1]
    spans = [(unit * a, unit * b) for a, b in zip(CUTS, CUTS[1:])]
    planes = [plane(val_g[None, :, a:b]) for a, b in spans]
    acts = across(acts)
    act_gram = gram_of(jnp.concatenate([mine, other]), acts)
    act_gram = act_gram[:rows] + shift(act_gram[rows:], "zl", 1)
    act_gram = exchange(
        jnp.broadcast_to(act_gram[None], (groups,) + act_gram.shape), "t"
    )
    act_gram = act_gram.reshape(-1, act_gram.shape[-1])

    grad_gram = 0.0
    for i, (a, b) in enumerate(spans):
        grad_gram = lax.optimization_barrier(grad_gram)
        grad_gram = grad_gram + gram_of(grad[:, a:b], across(planes[i]))
    folded = jnp.sum(act_gram * grad_gram, axis=1) * factor
    folded = exchange(folded.reshape(groups * layers, -1), ("t", "s"))
    return jnp.sum(folded, axis=0)


def solution(mesh):
    fine = Mesh(mesh.devices.reshape(4, 2, 8, 4, 2), ("x", "zl", "y", "t", "s"))
    dp = ("x", "zl", "y")
    in_specs = (
        P("s", (*dp, "t"), None),
        P("s", dp, "t"),
        P("s", dp, None),
        P("s", dp, "t"),
    )
    out_specs = P((*dp, "t", "s"))

    return jax.shard_map(local, mesh=fine, in_specs=in_specs, out_specs=out_specs, check_vma=False)
```

time: 755 us -> 153 us (0.20)
  waiting for transfers between devices: 664 us -> 44.8 us
  starting transfers between devices: 0.08 us -> 66.9 us
  blocking collectives: 56.2 us -> 24.6 us
  between operations: 13.8 us -> 0.28 us
  matrix products: 15.3 us -> 6.8 us
    all_gather x3 -> x0, waiting for transfers between devices: 664 us -> none  [the longest x1 300 us: local(): lax.all_gather(val_grad[0], 'dp', axis=0, tiled=True)]
    unnamed x1 -> x0, blocking collectives: 56.2 us -> none
    ppermute x0 -> x11, starting transfers between devices: none -> 34.6 us  [shift(): return lax.ppermute(block, axis, [(i, (i + by) % n) for i in range(n)])]
    all_to_all x0 -> x4, starting transfers between devices: none -> 32.3 us  [exchange(): return lax.all_to_all(blocks, axes, split_axis=0, concat_axis=0, tiled=True)]
    all_to_all x0 -> x1, blocking collectives: none -> 24.6 us  [exchange(): return lax.all_to_all(blocks, axes, split_axis=0, concat_axis=0, tiled=True)]
    all_to_all x0 -> x4, waiting for transfers between devices: none -> 23.8 us  [exchange(): return lax.all_to_all(blocks, axes, split_axis=0, concat_axis=0, tiled=True)]
    ppermute x0 -> x11, waiting for transfers between devices: none -> 21 us  [shift(): return lax.ppermute(block, axis, [(i, (i + by) % n) for i in range(n)])]
    dot_general x2 -> x3, matrix products: 15.3 us -> 6.8 us  [gram_of(): lax.dot_general(left, right, (((1,), (1,)), ((), ())), preferred_element_...]
  transfers between devices with their start and end apart: 3 -> 15, of which waited for: 3 -> 8; matrix products, arithmetic and copies ran while one was open for 2% -> 6% of each run, Pallas kernels for 0% -> 0%
where the time goes in v1:
time: 153 us; the launch traced here: 150 us
  starting transfers between devices  66.9 us (44%)
  waiting for transfers between devices  44.8 us (29%)
  blocking collectives  24.6 us (16%)
  matrix products  6.8 us (4%)
  local copies, waits for them, and re-layouts  6.01 us (4%)
    ppermute x11, starting transfers between devices, shift(): return lax.ppermute(block, axis, [(i, (i + by) % n) for i in range(n)])  34.6 us
    all_to_all x4, starting transfers between devices, exchange(): return lax.all_to_all(blocks, axes, split_axis=0, concat_axis=0, tiled=True)  32.3 us
    all_to_all x1, blocking collectives, exchange(): return lax.all_to_all(blocks, axes, split_axis=0, concat_axis=0, tiled=True)  24.6 us
    all_to_all x4, waiting for transfers between devices, exchange(): return lax.all_to_all(blocks, axes, split_axis=0, concat_axis=0, tiled=True)  23.8 us
    ppermute x11, waiting for transfers between devices, shift(): return lax.ppermute(block, axis, [(i, (i + by) % n) for i in range(n)])  21 us
    dot_general x3, matrix products, gram_of(): lax.dot_general(left, right, (((1,), (1,)), ((), ())), preferred_element_...  6.8 us
  transfers between devices with their start and end apart: 15, of which 8 were waited for; matrix products, arithmetic and copies ran while one was open for 6% of the time, Pallas kernels for 0%

profile of v1, /device:TPU:1, one launch (start us, length us, event | category | flops | bytes accessed | tf_op | source)
XLA Modules:
  0.0 150.0 jit_solution(3069957465356450506)
XLA Ops:
  0.0 0.0 copy-start
  0.0 0.9 fusion.47
  0.9 0.9 reshape.46
  1.8 9.6 %all-to-all-start.2 = ((bf16[16,4,3584]{2,1,0:T(4,128)(2,1)}), bf16[16,4,3584]{2,1,0:T(4,128)(2,1)S(1)}, u32[]{:S(2)}, u32[]{:S(2)}) async-start(bf16[16,4,3584]{2,1,0:T(4,128)(2,1)} %reshape.46), calls=%async_computation.2 | async-start | bytes 917504 | tf_op jit(solution)/shard_map/all_to_all | solution.py:19
  11.3 0.9 reshape_squeeze.3
  12.3 0.1 copy.11
  12.3 10.9 %all-to-all-done.2 = bf16[16,4,3584]{2,1,0:T(4,128)(2,1)S(1)} async-done(((bf16[16,4,3584]{2,1,0:T(4,128)(2,1)}), bf16[16,4,3584]{2,1,0:T(4,128)(2,1)S(1)}, u32[]{:S(2)}, u32[]{:S(2)}) %all-to-all-start.2) | async-done | bytes 458784 | tf_op jit(solution)/shard_map/all_to_all | solution.py:19
  23.3 1.0 broadcast_in_dim.4
  24.3 6.6 %all-to-all-start = ((bf16[16,4,4096]{2,1,0:T(4,128)(2,1)}), bf16[16,4,4096]{2,1,0:T(4,128)(2,1)S(1)}, u32[]{:S(2)}, u32[]{:S(2)}) async-start(bf16[16,4,4096]{2,1,0:T(4,128)(2,1)} %bitcast.3), calls=%async_computation | async-start | bytes 1048576 | tf_op jit(solution)/shard_map/all_to_all | solution.py:19
  30.9 12.8 %all-to-all-done = bf16[16,4,4096]{2,1,0:T(4,128)(2,1)S(1)} async-done(((bf16[16,4,4096]{2,1,0:T(4,128)(2,1)}), bf16[16,4,4096]{2,1,0:T(4,128)(2,1)S(1)}, u32[]{:S(2)}, u32[]{:S(2)}) %all-to-all-start) | async-done | bytes 524320 | tf_op jit(solution)/shard_map/all_to_all | solution.py:19
  43.7 0.9 reshape.48
  44.6 7.0 %all-to-all-start.3 = ((bf16[16,4,3584]{2,1,0:T(4,128)(2,1)}), bf16[16,4,3584]{2,1,0:T(4,128)(2,1)S(1)}, u32[]{:S(2)}, u32[]{:S(2)}) async-start(bf16[16,4,3584]{2,1,0:T(4,128)(2,1)} %reshape.48), calls=%async_computation.3 | async-start | bytes 917504 | tf_op jit(solution)/shard_map/all_to_all | solution.py:19
  51.6 0.0 copy-done
  51.6 0.1 dynamic-slice_bitcast_fusion.1
  51.7 3.3 %collective-permute-start = (bf16[64,4096]{1,0:T(8,128)(2,1)S(1)}, bf16[64,4096]{1,0:T(8,128)(2,1)}, u32[]{:S(2)}, u32[]{:S(2)}) collective-permute-start(bf16[64,4096]{1,0:T(8,128)(2,1)S(1)} %get-tuple-element.6), channel_id=1, source_target_pairs={{0,64},{64,0},{1,65},{65,1},{2,66},{66,2},{3,67},{67,3},{4,68},{68... | collective-permute-start | bytes 1572872 | tf_op jit(solution)/shard_map/ppermute | solution.py:24
  55.0 0.1 reshape.44
  55.1 3.1 %collective-permute-start.1 = (bf16[64,4096]{1,0:T(8,128)(2,1)S(1)}, bf16[64,4096]{1,0:T(8,128)(2,1)}, u32[]{:S(2)}, u32[]{:S(2)}) collective-permute-start(bf16[64,4096]{1,0:T(8,128)(2,1)S(1)} %reshape.44), channel_id=1, source_target_pairs={{0,128},{128,256},{256,384},{384,0},{1,129},{129,257},{257,385},{3... | collective-permute-start | bytes 1572872 | tf_op jit(solution)/shard_map/ppermute | solution.py:24
  58.3 3.4 %collective-permute-start.2 = (bf16[64,4096]{1,0:T(8,128)(2,1)S(1)}, bf16[64,4096]{1,0:T(8,128)(2,1)}, u32[]{:S(2)}, u32[]{:S(2)}) collective-permute-start(bf16[64,4096]{1,0:T(8,128)(2,1)S(1)} %reshape.44), channel_id=1, source_target_pairs={{0,384},{128,0},{256,128},{384,256},{1,385},{129,1},{257,129},{385... | collective-permute-start | bytes 1572872 | tf_op jit(solution)/shard_map/ppermute | solution.py:24
  61.7 3.4 %collective-permute-start.3 = (bf16[64,4096]{1,0:T(8,128)(2,1)S(1)}, bf16[64,4096]{1,0:T(8,128)(2,1)}, u32[]{:S(2)}, u32[]{:S(2)}) collective-permute-start(bf16[64,4096]{1,0:T(8,128)(2,1)S(1)} %reshape.44), channel_id=1, source_target_pairs={{0,256},{128,384},{256,0},{384,128},{1,257},{129,385},{257,1},{385... | collective-permute-start | bytes 1572872 | tf_op jit(solution)/shard_map/ppermute | solution.py:24
  65.1 0.1 reshape.47
  65.2 2.2 %collective-permute-start.5 = (bf16[64,3584]{1,0:T(8,128)(2,1)S(1)}, bf16[64,3584]{1,0:T(8,128)(2,1)}, u32[]{:S(2)}, u32[]{:S(2)}) collective-permute-start(bf16[64,3584]{1,0:T(8,128)(2,1)S(1)} %reshape.47), channel_id=1, source_target_pairs={{0,128},{128,256},{256,384},{384,0},{1,129},{129,257},{257,385},{3... | collective-permute-start | bytes 1376264 | tf_op jit(solution)/shard_map/ppermute | solution.py:24
  67.5 3.7 %collective-permute-done = bf16[64,4096]{1,0:T(8,128)(2,1)} collective-permute-done((bf16[64,4096]{1,0:T(8,128)(2,1)S(1)}, bf16[64,4096]{1,0:T(8,128)(2,1)}, u32[]{:S(2)}, u32[]{:S(2)}) %collective-permute-start) | collective-permute-done | bytes 524320 | tf_op jit(solution)/shard_map/ppermute | solution.py:24
  71.2 4.4 %collective-permute-start.6 = (bf16[64,3584]{1,0:T(8,128)(2,1)S(1)}, bf16[64,3584]{1,0:T(8,128)(2,1)}, u32[]{:S(2)}, u32[]{:S(2)}) collective-permute-start(bf16[64,3584]{1,0:T(8,128)(2,1)S(1)} %reshape.47), channel_id=1, source_target_pairs={{0,384},{128,0},{256,128},{384,256},{1,385},{129,1},{257,129},{385... | collective-permute-start | bytes 1376264 | tf_op jit(solution)/shard_map/ppermute | solution.py:24
  75.6 0.0 collective-permute-done.1
  75.6 2.4 %collective-permute-start.7 = (bf16[64,3584]{1,0:T(8,128)(2,1)S(1)}, bf16[64,3584]{1,0:T(8,128)(2,1)}, u32[]{:S(2)}, u32[]{:S(2)}) collective-permute-start(bf16[64,3584]{1,0:T(8,128)(2,1)S(1)} %reshape.47), channel_id=1, source_target_pairs={{0,256},{128,384},{256,0},{384,128},{1,257},{129,385},{257,1},{385... | collective-permute-start | bytes 1376264 | tf_op jit(solution)/shard_map/ppermute | solution.py:24
  78.0 0.0 all-to-all-done.3
  78.0 0.1 reshape.49
  78.2 0.0 collective-permute-done.2
  78.2 4.4 %collective-permute-start.10 = (bf16[64,3584]{1,0:T(8,128)(2,1)S(1)}, bf16[64,3584]{1,0:T(8,128)(2,1)S(1)}, u32[]{:S(2)}, u32[]{:S(2)}) collective-permute-start(bf16[64,3584]{1,0:T(8,128)(2,1)S(1)} %reshape.49), channel_id=1, source_target_pairs={{0,256},{128,384},{256,0},{384,128},{1,257},{129,385},{257,1},{385... | collective-permute-start | bytes 1376264 | tf_op jit(solution)/shard_map/ppermute | solution.py:24
  82.5 0.0 collective-permute-done.3
  82.5 4.1 %collective-permute-start.8 = (bf16[64,3584]{1,0:T(8,128)(2,1)S(1)}, bf16[64,3584]{1,0:T(8,128)(2,1)}, u32[]{:S(2)}, u32[]{:S(2)}) collective-permute-start(bf16[64,3584]{1,0:T(8,128)(2,1)S(1)} %reshape.49), channel_id=1, source_target_pairs={{0,128},{128,256},{256,384},{384,0},{1,129},{129,257},{257,385},{3... | collective-permute-start | bytes 1376264 | tf_op jit(solution)/shard_map/ppermute | solution.py:24
  86.6 0.0 copy-start.1
  86.6 2.5 %fusion = f32[128,256]{1,0:T(8,128)S(1)} fusion(bf16[64,4096]{1,0:T(8,128)(2,1)} %collective-permute-done.3, bf16[64,4096]{1,0:T(8,128)(2,1)} %collective-permute-done.2, bf16[64,4096]{1,0:T(8,128)(2,1)} %collective-permute-done.1, bf16[64,4096]{1,0:T(8,128)(2,1)S(1)} %reshape.44, bf16[64,4096]{1,0:T(8,128)(2,1)} %collective-permute-done, ...), kind=kOutput, calls=%fused_computation | convolution fusion | flops 278921216 | bytes 3276800 | tf_op jit(solution)/shard_map/dot_general | solution.py:13
  89.1 3.0 %collective-permute-done.5 = bf16[64,3584]{1,0:T(8,128)(2,1)} collective-permute-done((bf16[64,3584]{1,0:T(8,128)(2,1)S(1)}, bf16[64,3584]{1,0:T(8,128)(2,1)}, u32[]{:S(2)}, u32[]{:S(2)}) %collective-permute-start.5) | collective-permute-done | bytes 458784 | tf_op jit(solution)/shard_map/ppermute | solution.py:24
  92.2 2.1 %collective-permute-start.9 = (bf16[64,3584]{1,0:T(8,128)(2,1)S(1)}, bf16[64,3584]{1,0:T(8,128)(2,1)S(1)}, u32[]{:S(2)}, u32[]{:S(2)}) collective-permute-start(bf16[64,3584]{1,0:T(8,128)(2,1)S(1)} %reshape.49), channel_id=1, source_target_pairs={{0,384},{128,0},{256,128},{384,256},{1,385},{129,1},{257,129},{385... | collective-permute-start | bytes 1376264 | tf_op jit(solution)/shard_map/ppermute | solution.py:24
  94.2 2.2 %collective-permute-done.6 = bf16[64,3584]{1,0:T(8,128)(2,1)} collective-permute-done((bf16[64,3584]{1,0:T(8,128)(2,1)S(1)}, bf16[64,3584]{1,0:T(8,128)(2,1)}, u32[]{:S(2)}, u32[]{:S(2)}) %collective-permute-start.6) | collective-permute-done | bytes 458784 | tf_op jit(solution)/shard_map/ppermute | solution.py:24
  96.5 1.9 %collective-permute-start.4 = (f32[64,256]{1,0:T(8,128)S(1)}, f32[64,256]{1,0:T(8,128)S(1)}, u32[]{:S(2)}, u32[]{:S(2)}) collective-permute-start(f32[64,256]{1,0:T(8,128)S(1)} %slice.25), channel_id=1, source_target_pairs={{0,64},{64,0},{1,65},{65,1},{2,66},{66,2},{3,67},{67,3},{4,68},{68... | collective-permute-start | bytes 196616 | tf_op jit(solution)/shard_map/ppermute | solution.py:24
  98.4 3.5 %collective-permute-done.7 = bf16[64,3584]{1,0:T(8,128)(2,1)} collective-permute-done((bf16[64,3584]{1,0:T(8,128)(2,1)S(1)}, bf16[64,3584]{1,0:T(8,128)(2,1)}, u32[]{:S(2)}, u32[]{:S(2)}) %collective-permute-start.7) | collective-permute-done | bytes 458784 | tf_op jit(solution)/shard_map/ppermute | solution.py:24
  101.9 0.0 copy-done.1
  101.9 2.0 %fusion.36 = f32[256,256]{0,1:T(8,128)S(1)} fusion(bf16[256,7168]{1,0:T(8,128)(2,1)S(1)} %bitcast.19, bf16[64,3584]{1,0:T(8,128)(2,1)} %collective-permute-done.7, bf16[64,3584]{1,0:T(8,128)(2,1)} %collective-permute-done.6, bf16[64,3584]{1,0:T(8,128)(2,1)} %collective-permute-done.5, bf16[64,3584]{1,0:T(8,128)(2,1)S(1)} %reshape.47, f32[]{:T(128)} %constant.18.clone.1), kind=kOutput, calls=%fused_computation.28 | convolution fusion | flops 477167616 | bytes 3932164 | tf_op jit(solution)/shard_map/dot_general | solution.py:13
  103.9 0.0 collective-permute-done.4
  103.9 0.7 broadcast_in_dim.5
  104.6 9.1 %all-to-all-start.1 = ((f32[4,64,256]{2,1,0:T(8,128)}), f32[4,64,256]{2,1,0:T(8,128)S(1)}, u32[]{:S(2)}, u32[]{:S(2)}) async-start(f32[4,64,256]{2,1,0:T(8,128)} %broadcast_in_dim.5), calls=%async_computation.1 | async-start | bytes 524288 | tf_op jit(solution)/shard_map/all_to_all | solution.py:19
  113.7 0.0 collective-permute-done.10
  113.8 7.8 %collective-permute-done.8 = bf16[64,3584]{1,0:T(8,128)(2,1)} collective-permute-done((bf16[64,3584]{1,0:T(8,128)(2,1)S(1)}, bf16[64,3584]{1,0:T(8,128)(2,1)}, u32[]{:S(2)}, u32[]{:S(2)}) %collective-permute-start.8) | collective-permute-done | bytes 458784 | tf_op jit(solution)/shard_map/ppermute | solution.py:24
  121.6 0.6 collective-permute-done.9
  122.2 2.3 %fusion.26 = f32[256,256]{0,1:T(8,128)S(1)} fusion(bf16[256,7168]{1,0:T(8,128)(2,1)} %bitcast.18, bf16[64,3584]{1,0:T(8,128)(2,1)S(1)} %collective-permute-done.10, bf16[64,3584]{1,0:T(8,128)(2,1)S(1)} %collective-permute-done.9, bf16[64,3584]{1,0:T(8,128)(2,1)} %collective-permute-done.8, bf16[64,3584]{1,0:T(8,128)(2,1)S(1)} %reshape.49), kind=kOutput, calls=%fused_computation.26 | convolution fusion | flops 477102080 | bytes 3932160 | tf_op jit(solution)/shard_map/dot_general | solution.py:13
  124.6 0.0 all-to-all-done.1
  124.6 0.1 copy.12
  124.7 0.1 multiply_reduce_fusion
  124.8 0.1 mul.31
  124.9 24.6 %all_to_all.26 = f32[8,1,32]{2,1,0:T(1,128)S(1)} all-to-all(f32[8,1,32]{2,1,0:T(1,128)S(1)} %mul.31), channel_id=1, replica_groups=mesh['x'=4,'zl'=2,'y'=8,'t'=4,'s'=2] {'t','s'}, dimensions={0} | all-to-all | bytes 2048 | tf_op jit(solution)/shard_map/all_to_all | solution.py:19
  149.5 0.5 reduce_sum.19
  (3 shorter events, 0.0 us)
Async XLA Ops:
  0.0 51.6 %copy-start = (bf16[1,64,8192]{2,1,0:T(8,128)(2,1)S(1)}, bf16[1,64,8192]{2,1,0:T(8,128)(2,1)}, u32[]{:S(2)}) copy-start(bf16[1,64,8192]{2,1,0:T(8,128)(2,1)} %param.4) | copy-start | bytes 3145732
  1.8 21.5 %all-to-all-start.2 = ((bf16[16,4,3584]{2,1,0:T(4,128)(2,1)}), bf16[16,4,3584]{2,1,0:T(4,128)(2,1)S(1)}, u32[]{:S(2)}, u32[]{:S(2)}) async-start(bf16[16,4,3584]{2,1,0:T(4,128)(2,1)} %reshape.46), calls=%async_computation.2 | async-start | bytes 917504 | tf_op jit(solution)/shard_map/all_to_all | solution.py:19
  24.3 19.4 %all-to-all-start = ((bf16[16,4,4096]{2,1,0:T(4,128)(2,1)}), bf16[16,4,4096]{2,1,0:T(4,128)(2,1)S(1)}, u32[]{:S(2)}, u32[]{:S(2)}) async-start(bf16[16,4,4096]{2,1,0:T(4,128)(2,1)} %bitcast.3), calls=%async_computation | async-start | bytes 1048576 | tf_op jit(solution)/shard_map/all_to_all | solution.py:19
  44.6 33.4 %all-to-all-start.3 = ((bf16[16,4,3584]{2,1,0:T(4,128)(2,1)}), bf16[16,4,3584]{2,1,0:T(4,128)(2,1)S(1)}, u32[]{:S(2)}, u32[]{:S(2)}) async-start(bf16[16,4,3584]{2,1,0:T(4,128)(2,1)} %reshape.48), calls=%async_computation.3 | async-start | bytes 917504 | tf_op jit(solution)/shard_map/all_to_all | solution.py:19
  51.7 19.5 %collective-permute-start = (bf16[64,4096]{1,0:T(8,128)(2,1)S(1)}, bf16[64,4096]{1,0:T(8,128)(2,1)}, u32[]{:S(2)}, u32[]{:S(2)}) collective-permute-start(bf16[64,4096]{1,0:T(8,128)(2,1)S(1)} %get-tuple-element.6), channel_id=1, source_target_pairs={{0,64},{64,0},{1,65},{65,1},{2,66},{66,2},{3,67},{67,3},{4,68},{68... | collective-permute-start | bytes 1572872 | tf_op jit(solution)/shard_map/ppermute | solution.py:24
  55.1 20.4 %collective-permute-start.1 = (bf16[64,4096]{1,0:T(8,128)(2,1)S(1)}, bf16[64,4096]{1,0:T(8,128)(2,1)}, u32[]{:S(2)}, u32[]{:S(2)}) collective-permute-start(bf16[64,4096]{1,0:T(8,128)(2,1)S(1)} %reshape.44), channel_id=1, source_target_pairs={{0,128},{128,256},{256,384},{384,0},{1,129},{129,257},{257,385},{3... | collective-permute-start | bytes 1572872 | tf_op jit(solution)/shard_map/ppermute | solution.py:24
  58.3 19.9 %collective-permute-start.2 = (bf16[64,4096]{1,0:T(8,128)(2,1)S(1)}, bf16[64,4096]{1,0:T(8,128)(2,1)}, u32[]{:S(2)}, u32[]{:S(2)}) collective-permute-start(bf16[64,4096]{1,0:T(8,128)(2,1)S(1)} %reshape.44), channel_id=1, source_target_pairs={{0,384},{128,0},{256,128},{384,256},{1,385},{129,1},{257,129},{385... | collective-permute-start | bytes 1572872 | tf_op jit(solution)/shard_map/ppermute | solution.py:24
  61.7 20.9 %collective-permute-start.3 = (bf16[64,4096]{1,0:T(8,128)(2,1)S(1)}, bf16[64,4096]{1,0:T(8,128)(2,1)}, u32[]{:S(2)}, u32[]{:S(2)}) collective-permute-start(bf16[64,4096]{1,0:T(8,128)(2,1)S(1)} %reshape.44), channel_id=1, source_target_pairs={{0,256},{128,384},{256,0},{384,128},{1,257},{129,385},{257,1},{385... | collective-permute-start | bytes 1572872 | tf_op jit(solution)/shard_map/ppermute | solution.py:24
  65.2 26.9 %collective-permute-start.5 = (bf16[64,3584]{1,0:T(8,128)(2,1)S(1)}, bf16[64,3584]{1,0:T(8,128)(2,1)}, u32[]{:S(2)}, u32[]{:S(2)}) collective-permute-start(bf16[64,3584]{1,0:T(8,128)(2,1)S(1)} %reshape.47), channel_id=1, source_target_pairs={{0,128},{128,256},{256,384},{384,0},{1,129},{129,257},{257,385},{3... | collective-permute-start | bytes 1376264 | tf_op jit(solution)/shard_map/ppermute | solution.py:24
  71.2 25.3 %collective-permute-start.6 = (bf16[64,3584]{1,0:T(8,128)(2,1)S(1)}, bf16[64,3584]{1,0:T(8,128)(2,1)}, u32[]{:S(2)}, u32[]{:S(2)}) collective-permute-start(bf16[64,3584]{1,0:T(8,128)(2,1)S(1)} %reshape.47), channel_id=1, source_target_pairs={{0,384},{128,0},{256,128},{384,256},{1,385},{129,1},{257,129},{385... | collective-permute-start | bytes 1376264 | tf_op jit(solution)/shard_map/ppermute | solution.py:24
  75.6 26.3 %collective-permute-start.7 = (bf16[64,3584]{1,0:T(8,128)(2,1)S(1)}, bf16[64,3584]{1,0:T(8,128)(2,1)}, u32[]{:S(2)}, u32[]{:S(2)}) collective-permute-start(bf16[64,3584]{1,0:T(8,128)(2,1)S(1)} %reshape.47), channel_id=1, source_target_pairs={{0,256},{128,384},{256,0},{384,128},{1,257},{129,385},{257,1},{385... | collective-permute-start | bytes 1376264 | tf_op jit(solution)/shard_map/ppermute | solution.py:24
  78.2 35.6 %collective-permute-start.10 = (bf16[64,3584]{1,0:T(8,128)(2,1)S(1)}, bf16[64,3584]{1,0:T(8,128)(2,1)S(1)}, u32[]{:S(2)}, u32[]{:S(2)}) collective-permute-start(bf16[64,3584]{1,0:T(8,128)(2,1)S(1)} %reshape.49), channel_id=1, source_target_pairs={{0,256},{128,384},{256,0},{384,128},{1,257},{129,385},{257,1},{385... | collective-permute-start | bytes 1376264 | tf_op jit(solution)/shard_map/ppermute | solution.py:24
  82.5 39.1 %collective-permute-start.8 = (bf16[64,3584]{1,0:T(8,128)(2,1)S(1)}, bf16[64,3584]{1,0:T(8,128)(2,1)}, u32[]{:S(2)}, u32[]{:S(2)}) collective-permute-start(bf16[64,3584]{1,0:T(8,128)(2,1)S(1)} %reshape.49), channel_id=1, source_target_pairs={{0,128},{128,256},{256,384},{384,0},{1,129},{129,257},{257,385},{3... | collective-permute-start | bytes 1376264 | tf_op jit(solution)/shard_map/ppermute | solution.py:24
  86.6 15.3 %copy-start.1 = (bf16[1,256,7168]{2,1,0:T(8,128)(2,1)S(1)}, bf16[1,256,7168]{2,1,0:T(8,128)(2,1)}, u32[]{:S(2)}) copy-start(bf16[1,256,7168]{2,1,0:T(8,128)(2,1)} %param.5) | copy-start | bytes 11010052
  92.2 30.1 %collective-permute-start.9 = (bf16[64,3584]{1,0:T(8,128)(2,1)S(1)}, bf16[64,3584]{1,0:T(8,128)(2,1)S(1)}, u32[]{:S(2)}, u32[]{:S(2)}) collective-permute-start(bf16[64,3584]{1,0:T(8,128)(2,1)S(1)} %reshape.49), channel_id=1, source_target_pairs={{0,384},{128,0},{256,128},{384,256},{1,385},{129,1},{257,129},{385... | collective-permute-start | bytes 1376264 | tf_op jit(solution)/shard_map/ppermute | solution.py:24
  96.5 7.4 %collective-permute-start.4 = (f32[64,256]{1,0:T(8,128)S(1)}, f32[64,256]{1,0:T(8,128)S(1)}, u32[]{:S(2)}, u32[]{:S(2)}) collective-permute-start(f32[64,256]{1,0:T(8,128)S(1)} %slice.25), channel_id=1, source_target_pairs={{0,64},{64,0},{1,65},{65,1},{2,66},{66,2},{3,67},{67,3},{4,68},{68... | collective-permute-start | bytes 196616 | tf_op jit(solution)/shard_map/ppermute | solution.py:24
  104.6 19.9 %all-to-all-start.1 = ((f32[4,64,256]{2,1,0:T(8,128)}), f32[4,64,256]{2,1,0:T(8,128)S(1)}, u32[]{:S(2)}, u32[]{:S(2)}) async-start(f32[4,64,256]{2,1,0:T(8,128)} %broadcast_in_dim.5), calls=%async_computation.1 | async-start | bytes 524288 | tf_op jit(solution)/shard_map/all_to_all | solution.py:19

commit v2 on v1

v2 whole, which is shorter than its diff:
```python
import math

import jax
import jax.numpy as jnp
from jax import lax
from jax.sharding import Mesh, PartitionSpec as P


CUTS = (0, 4, 14)


def gram_of(left, right):
    return lax.dot_general(
        left, right, (((1,), (1,)), ((), ())), preferred_element_type=jnp.float32
    )


def exchange(blocks, axes):
    return lax.all_to_all(blocks, axes, split_axis=0, concat_axis=0, tiled=True)


def plane(blocks):
    pair, half = lax.axis_size("zl"), lax.axis_size("yh")
    shape = blocks.shape[2:]
    blocks = jnp.broadcast_to(blocks[:, None], (pair, half, pair) + shape)
    blocks = blocks.reshape((-1,) + shape)
    rows = exchange(blocks, ("zl", "yh", "yl"))
    return rows.reshape(-1, shape[1])


def across(rows):
    n = lax.axis_size("x")
    moved = []
    for by in (1, -1, 2):
        pairs = [(j, (j + by) % n) for j in range(n)]
        moved.append(lax.ppermute(rows, "x", pairs))
    return jnp.concatenate([rows, *moved])


def local(train_act, train_grad, val_act, val_grad):
    own, grad, val_a, val_g = train_act[0], train_grad[0], val_act[0], val_grad[0]
    groups, layers = lax.axis_size("t"), lax.axis_size("s")
    team = ("zl", "yl")
    me, size = lax.axis_index(team), lax.axis_size(team)
    rows, width = own.shape
    hidden = grad.shape[1] * groups
    part = width // size
    val_total = val_a.shape[0] * lax.axis_size(("x", "zl", "yh", "yl"))
    factor = 1.0 / math.sqrt(width * hidden * val_total)
    unit = grad.shape[1] // CUTS[-1]
    spans = [(unit * a, unit * b) for a, b in zip(CUTS, CUTS[1:])]

    first = val_g[:, : spans[0][1]]
    quarters = [val_a[:, q * part : (q + 1) * part] for q in range(size)]
    blocks = jnp.stack([jnp.concatenate([q, first], axis=1) for q in quarters])
    planes = [plane(blocks.reshape((2, 2) + blocks.shape[1:]))]

    pieces = []
    for j in range(size):
        piece = lax.dynamic_slice_in_dim(own, (me ^ j) * part, part, 1)
        if j:
            piece = lax.ppermute(piece, team, [(i, i ^ j) for i in range(size)])
        pieces.append(piece)
    for i, (a, b) in enumerate(spans[1:], 1):
        val = val_g[None, None, :, a:b]
        planes.append(plane(jnp.broadcast_to(val, (2, 2) + val.shape[2:])))

    acts = across(planes[0][:, :part])
    planes[0] = planes[0][:, part:]
    act_gram = gram_of(jnp.concatenate(pieces), acts)
    act_gram = jnp.concatenate(
        [
            lax.dynamic_slice_in_dim(act_gram, (me ^ j) * rows, rows, 0)
            for j in range(size)
        ]
    )
    act_gram = exchange(act_gram.reshape(size, rows, -1), team)
    act_gram = jnp.sum(act_gram, axis=0)
    act_gram = lax.all_gather(act_gram, "t", axis=0, tiled=True)

    grad_gram = 0.0
    for i, (a, b) in enumerate(spans):
        grad_gram = lax.optimization_barrier(grad_gram)
        grad_gram = grad_gram + gram_of(grad[:, a:b], across(planes[i]))
    folded = jnp.sum(act_gram * grad_gram, axis=1) * factor
    folded = exchange(folded.reshape(groups * layers, -1), ("t", "s"))
    return jnp.sum(folded, axis=0)


def solution(mesh):
    axes = ("x", "zl", "yh", "yl", "t", "s")
    fine = Mesh(mesh.devices.reshape(4, 2, 4, 2, 4, 2), axes)
    dp = axes[:4]
    in_specs = (
        P("s", (*dp, "t"), None),
        P("s", dp, "t"),
        P("s", dp, None),
        P("s", dp, "t"),
    )
    out_specs = P((*dp, "t", "s"))

    return jax.shard_map(local, mesh=fine, in_specs=in_specs, out_specs=out_specs, check_vma=False)
```

time: 153 us -> 136 us (0.89)
  the two profiles are of different devices: /device:TPU:1 before, /device:TPU:22 now
where the time goes in v2:
time: 136 us; the launch traced here: 135 us
  starting transfers between devices  65.2 us (48%)
  blocking collectives  30.6 us (22%)
  waiting for transfers between devices  25.5 us (19%)
  matrix products  6.71 us (5%)
  local copies, waits for them, and re-layouts  4.96 us (4%)
  other arithmetic  1.5 us (1%)
    ppermute x9, starting transfers between devices, across(): moved.append(lax.ppermute(rows, 'x', pairs))  29.5 us
    all_to_all x3, starting transfers between devices, exchange(): return lax.all_to_all(blocks, axes, split_axis=0, concat_axis=0, tiled=True)  26.5 us
    all_gather x1, blocking collectives, local(): act_gram = lax.all_gather(act_gram, 't', axis=0, tiled=True)  18.2 us
    all_to_all x3, waiting for transfers between devices, exchange(): return lax.all_to_all(blocks, axes, split_axis=0, concat_axis=0, tiled=True)  17.9 us
    all_to_all x1, blocking collectives, exchange(): return lax.all_to_all(blocks, axes, split_axis=0, concat_axis=0, tiled=True)  12.4 us
    ppermute x3, starting transfers between devices, local(): piece = lax.ppermute(piece, team, [(i, i ^ j) for i in range(size)])  9.22 us
    ppermute x3, waiting for transfers between devices, local(): piece = lax.ppermute(piece, team, [(i, i ^ j) for i in range(size)])  7.58 us
    dot_general x3, matrix products, gram_of(): lax.dot_general(left, right, (((1,), (1,)), ((), ())), preferred_element_...  6.71 us
  transfers between devices with their start and end apart: 15, of which 3 were waited for; matrix products, arithmetic and copies ran while one was open for 4% of the time, Pallas kernels for 0%

profile of v2, /device:TPU:22, one launch (start us, length us, event | category | flops | bytes accessed | tf_op | source)
XLA Modules:
  0.0 134.8 jit_solution(5682431599319619550)
XLA Ops:
  0.0 0.0 copy-start.1
  0.0 0.8 fusion.46
  0.8 0.7 slice.41
  1.5 0.1 fusion.38
  1.6 0.0 copy-start
  1.6 0.1 pad_maximum_fusion.1
  1.7 1.0 broadcast_in_dim.9
  2.7 9.3 %all-to-all-start = ((bf16[16,4,4096]{2,1,0:T(4,128)(2,1)}), bf16[16,4,4096]{2,1,0:T(4,128)(2,1)S(1)}, u32[]{:S(2)}, u32[]{:S(2)}) async-start(bf16[16,4,4096]{2,1,0:T(4,128)(2,1)} %bitcast.11), calls=%async_computation | async-start | bytes 1048576 | tf_op jit(solution)/shard_map/all_to_all | solution.py:19
  12.0 0.0 copy-done.1
  12.0 14.6 %all-to-all-done = bf16[16,4,4096]{2,1,0:T(4,128)(2,1)S(1)} async-done(((bf16[16,4,4096]{2,1,0:T(4,128)(2,1)}), bf16[16,4,4096]{2,1,0:T(4,128)(2,1)S(1)}, u32[]{:S(2)}, u32[]{:S(2)}) %all-to-all-start) | async-done | bytes 524320 | tf_op jit(solution)/shard_map/all_to_all | solution.py:19
  26.6 1.0 reshape.39
  27.6 5.6 %all-to-all-start.2 = ((bf16[16,4,5120]{2,1,0:T(4,128)(2,1)}), bf16[16,4,5120]{2,1,0:T(4,128)(2,1)S(1)}, u32[]{:S(2)}, u32[]{:S(2)}) async-start(bf16[16,4,5120]{2,1,0:T(4,128)(2,1)} %reshape.39), calls=%async_computation.2 | async-start | bytes 1310720 | tf_op jit(solution)/shard_map/all_to_all | solution.py:19
  33.3 0.0 copy-done
  33.3 0.1 dynamic-slice_bitcast_fusion.3
  33.4 3.4 %collective-permute-start = (bf16[64,2048]{1,0:T(8,128)(2,1)S(1)}, bf16[64,2048]{1,0:T(8,128)(2,1)}, u32[]{:S(2)}, u32[]{:S(2)}) collective-permute-start(bf16[64,2048]{1,0:T(8,128)(2,1)S(1)} %get-tuple-element.6), channel_id=1, source_target_pairs={{0,8},{8,0},{64,72},{72,64},{1,9},{9,1},{65,73},{73,65},{2,10},{10... | collective-permute-start | bytes 786440 | tf_op jit(solution)/shard_map/ppermute | solution.py:62
  36.8 3.4 %collective-permute-start.1 = (bf16[64,2048]{1,0:T(8,128)(2,1)S(1)}, bf16[64,2048]{1,0:T(8,128)(2,1)}, u32[]{:S(2)}, u32[]{:S(2)}) collective-permute-start(bf16[64,2048]{1,0:T(8,128)(2,1)S(1)} %get-tuple-element.8), channel_id=1, source_target_pairs={{0,64},{8,72},{64,0},{72,8},{1,65},{9,73},{65,1},{73,9},{2,66},{10... | collective-permute-start | bytes 786440 | tf_op jit(solution)/shard_map/ppermute | solution.py:62
  40.1 2.5 %collective-permute-start.2 = (bf16[64,2048]{1,0:T(8,128)(2,1)S(1)}, bf16[64,2048]{1,0:T(8,128)(2,1)}, u32[]{:S(2)}, u32[]{:S(2)}) collective-permute-start(bf16[64,2048]{1,0:T(8,128)(2,1)S(1)} %get-tuple-element.7), channel_id=1, source_target_pairs={{0,72},{8,64},{64,8},{72,0},{1,73},{9,65},{65,9},{73,1},{2,74},{10... | collective-permute-start | bytes 786440 | tf_op jit(solution)/shard_map/ppermute | solution.py:62
  42.6 0.1 reshape.37
  42.8 2.4 %collective-permute-start.3 = (bf16[64,2048]{1,0:T(8,128)(2,1)S(1)}, bf16[64,2048]{1,0:T(8,128)(2,1)}, u32[]{:S(2)}, u32[]{:S(2)}) collective-permute-start(bf16[64,2048]{1,0:T(8,128)(2,1)S(1)} %get-tuple-element.10), channel_id=1, source_target_pairs={{0,128},{128,256},{256,384},{384,0},{1,129},{129,257},{257,385},{3... | collective-permute-start | bytes 786440 | tf_op jit(solution)/shard_map/ppermute | solution.py:36
  45.2 3.5 %collective-permute-start.4 = (bf16[64,2048]{1,0:T(8,128)(2,1)S(1)}, bf16[64,2048]{1,0:T(8,128)(2,1)S(1)}, u32[]{:S(2)}, u32[]{:S(2)}) collective-permute-start(bf16[64,2048]{1,0:T(8,128)(2,1)S(1)} %get-tuple-element.10), channel_id=1, source_target_pairs={{0,384},{128,0},{256,128},{384,256},{1,385},{129,1},{257,129},{385... | collective-permute-start | bytes 786440 | tf_op jit(solution)/shard_map/ppermute | solution.py:36
  48.7 7.6 %collective-permute-done = bf16[64,2048]{1,0:T(8,128)(2,1)} collective-permute-done((bf16[64,2048]{1,0:T(8,128)(2,1)S(1)}, bf16[64,2048]{1,0:T(8,128)(2,1)}, u32[]{:S(2)}, u32[]{:S(2)}) %collective-permute-start) | collective-permute-done | bytes 262176 | tf_op jit(solution)/shard_map/ppermute | solution.py:62
  56.2 3.3 %collective-permute-start.5 = (bf16[64,2048]{1,0:T(8,128)(2,1)S(1)}, bf16[64,2048]{1,0:T(8,128)(2,1)}, u32[]{:S(2)}, u32[]{:S(2)}) collective-permute-start(bf16[64,2048]{1,0:T(8,128)(2,1)S(1)} %get-tuple-element.10), channel_id=1, source_target_pairs={{0,256},{128,384},{256,0},{384,128},{1,257},{129,385},{257,1},{385... | collective-permute-start | bytes 786440 | tf_op jit(solution)/shard_map/ppermute | solution.py:36
  59.5 0.0 collective-permute-done.1
  59.5 4.0 %collective-permute-start.6 = (bf16[64,2048]{1,0:T(8,128)(2,1)S(1)}, bf16[64,2048]{1,0:T(8,128)(2,1)S(1)}, u32[]{:S(2)}, u32[]{:S(2)}) collective-permute-start(bf16[64,2048]{1,0:T(8,128)(2,1)S(1)} %get-tuple-element.9), channel_id=1, source_target_pairs={{0,128},{128,256},{256,384},{384,0},{1,129},{129,257},{257,385},{3... | collective-permute-start | bytes 786440 | tf_op jit(solution)/shard_map/ppermute | solution.py:36
  63.6 0.0 all-to-all-done.2
  63.6 0.1 reshape.40
  63.7 0.0 collective-permute-done.2
  63.8 1.9 %collective-permute-start.7 = (bf16[64,2048]{1,0:T(8,128)(2,1)S(1)}, bf16[64,2048]{1,0:T(8,128)(2,1)S(1)}, u32[]{:S(2)}, u32[]{:S(2)}) collective-permute-start(bf16[64,2048]{1,0:T(8,128)(2,1)S(1)} %get-tuple-element.9), channel_id=1, source_target_pairs={{0,384},{128,0},{256,128},{384,256},{1,385},{129,1},{257,129},{385... | collective-permute-start | bytes 786440 | tf_op jit(solution)/shard_map/ppermute | solution.py:36
  65.7 0.0 collective-permute-done.3
  65.7 4.0 %collective-permute-start.8 = (bf16[64,2048]{1,0:T(8,128)(2,1)S(1)}, bf16[64,2048]{1,0:T(8,128)(2,1)}, u32[]{:S(2)}, u32[]{:S(2)}) collective-permute-start(bf16[64,2048]{1,0:T(8,128)(2,1)S(1)} %get-tuple-element.9), channel_id=1, source_target_pairs={{0,256},{128,384},{256,0},{384,128},{1,257},{129,385},{257,1},{385... | collective-permute-start | bytes 786440 | tf_op jit(solution)/shard_map/ppermute | solution.py:36
  69.7 0.0 collective-permute-done.4
  69.7 0.0 copy-start.2
  69.7 3.9 %collective-permute-start.10 = (bf16[64,5120]{1,0:T(8,128)(2,1)S(1)}, bf16[64,5120]{1,0:T(8,128)(2,1)S(1)}, u32[]{:S(2)}, u32[]{:S(2)}) collective-permute-start(bf16[64,5120]{1,0:T(8,128)(2,1)S(1)} %reshape.40), channel_id=1, source_target_pairs={{0,384},{128,0},{256,128},{384,256},{1,385},{129,1},{257,129},{385... | collective-permute-start | bytes 1966088 | tf_op jit(solution)/shard_map/ppermute | solution.py:36
  73.6 0.0 collective-permute-done.5
  73.6 2.5 %collective-permute-start.11 = (bf16[64,5120]{1,0:T(8,128)(2,1)S(1)}, bf16[64,5120]{1,0:T(8,128)(2,1)}, u32[]{:S(2)}, u32[]{:S(2)}) collective-permute-start(bf16[64,5120]{1,0:T(8,128)(2,1)S(1)} %reshape.40), channel_id=1, source_target_pairs={{0,256},{128,384},{256,0},{384,128},{1,257},{129,385},{257,1},{385... | collective-permute-start | bytes 1966088 | tf_op jit(solution)/shard_map/ppermute | solution.py:36
  76.2 0.0 copy-done.2
  76.2 1.8 %fusion.16 = f32[256,256]{1,0:T(8,128)S(1)} fusion(bf16[64,2048]{1,0:T(8,128)(2,1)} %collective-permute-done.2, bf16[64,2048]{1,0:T(8,128)(2,1)} %collective-permute-done.1, bf16[64,2048]{1,0:T(8,128)(2,1)} %collective-permute-done, bf16[64,2048]{1,0:T(8,128)(2,1)S(1)} %get-tuple-element.5, bf16[64,2048]{1,0:T(8,128)(2,1)} %collective-permute-done.5, ...), kind=kOutput, calls=%fused_computation.13 | convolution fusion | flops 276824064 | bytes 2359296 | tf_op jit(solution)/shard_map/dot_general | solution.py:13
  78.0 0.0 collective-permute-done.6
  78.0 4.0 %collective-permute-start.9 = (bf16[64,5120]{1,0:T(8,128)(2,1)S(1)}, bf16[64,5120]{1,0:T(8,128)(2,1)}, u32[]{:S(2)}, u32[]{:S(2)}) collective-permute-start(bf16[64,5120]{1,0:T(8,128)(2,1)S(1)} %reshape.40), channel_id=1, source_target_pairs={{0,128},{128,256},{256,384},{384,0},{1,129},{129,257},{257,385},{3... | collective-permute-start | bytes 1966088 | tf_op jit(solution)/shard_map/ppermute | solution.py:36
  82.0 0.7 pad_maximum_fusion
  82.8 11.6 %all-to-all-start.1 = ((f32[4,64,256]{2,1,0:T(8,128)}), f32[4,64,256]{2,1,0:T(8,128)S(1)}, u32[]{:S(2)}, u32[]{:S(2)}) async-start(f32[4,64,256]{2,1,0:T(8,128)} %bitcast.12), calls=%async_computation.1 | async-start | bytes 524288 | tf_op jit(solution)/shard_map/all_to_all | solution.py:19
  94.4 0.0 collective-permute-done.7
  94.4 0.0 copy-start.3
  94.4 0.0 collective-permute-done.8
  94.4 0.7 copy-done.3
  95.1 1.9 %fusion.14 = f32[256,256]{0,1:T(8,128)S(1)} fusion(bf16[256,7168]{1,0:T(8,128)(2,1)} %bitcast.32, bf16[64,2048]{1,0:T(8,128)(2,1)} %collective-permute-done.8, bf16[64,2048]{1,0:T(8,128)(2,1)} %copy-done.3, bf16[64,2048]{1,0:T(8,128)(2,1)S(1)} %collective-permute-done.6, bf16[64,2048]{1,0:T(8,128)(2,1)S(1)} %get-tuple-element.9, f32[]{:T(128)} %constant.32.clone.1), kind=kOutput, calls=%fused_computation.11 | convolution fusion | flops 272695296 | bytes 2359808 | tf_op jit(solution)/shard_map/dot_general | solution.py:13
  97.0 3.3 %all-to-all-done.1 = f32[4,64,256]{2,1,0:T(8,128)S(1)} async-done(((f32[4,64,256]{2,1,0:T(8,128)}), f32[4,64,256]{2,1,0:T(8,128)S(1)}, u32[]{:S(2)}, u32[]{:S(2)}) %all-to-all-start.1) | async-done | bytes 262176 | tf_op jit(solution)/shard_map/all_to_all | solution.py:19
  100.3 18.2 %all_gather.3 = f32[256,256]{1,0:T(8,128)S(1)} all-gather(f32[64,256]{1,0:T(8,128)S(1)} %reduce_sum.27), channel_id=1, replica_groups=mesh['x'=4,'zl'=2,'yh'=4,'yl'=2,'t'=4,'s'=2] {'t'}, dimensions={0}, use_global_device_ids=true | all-gather | bytes 327680 | tf_op jit(solution)/shard_map/all_gather | solution.py:79
  118.5 0.1 copy.7
  118.6 0.0 collective-permute-done.10
  118.6 0.0 collective-permute-done.11
  118.6 0.0 collective-permute-done.9
  118.6 3.0 %fusion.9 = f32[256,256]{0,1:T(8,128)S(1)} fusion(bf16[256,7168]{1,0:T(8,128)(2,1)} %bitcast.33, bf16[64,5120]{1,0:T(8,128)(2,1)} %collective-permute-done.11, bf16[64,5120]{1,0:T(8,128)(2,1)S(1)} %collective-permute-done.10, bf16[64,5120]{1,0:T(8,128)(2,1)} %collective-permute-done.9, bf16[64,5120]{1,0:T(8,128)(2,1)S(1)} %reshape.40), kind=kOutput, calls=%fused_computation.9 | convolution fusion | flops 681574400 | bytes 5505024 | tf_op jit(solution)/shard_map/dot_general | solution.py:13
  121.7 0.1 multiply_reduce_fusion
  121.7 0.1 mul.59
  121.8 12.4 %all_to_all.21 = f32[8,1,32]{2,1,0:T(1,128)S(1)} all-to-all(f32[8,1,32]{2,1,0:T(1,128)S(1)} %mul.59), channel_id=1, replica_groups=mesh['x'=4,'zl'=2,'yh'=4,'yl'=2,'t'=4,'s'=2] {'t','s'}, dimensions={0} | all-to-all | bytes 2048 | tf_op jit(solution)/shard_map/all_to_all | solution.py:19
  134.2 0.5 reduce_sum.29
  (5 shorter events, 0.1 us)
Async XLA Ops:
  0.0 12.0 %copy-start.1 = (bf16[1,4,7168]{2,1,0:T(4,128)(2,1)S(1)}, bf16[1,4,7168]{2,1,0:T(4,128)(2,1)}, u32[]{:S(2)}) copy-start(bf16[1,4,7168]{2,1,0:T(4,128)(2,1)} %param.7) | copy-start | bytes 172036
  1.6 31.7 %copy-start = (bf16[1,64,8192]{2,1,0:T(8,128)(2,1)S(1)}, bf16[1,64,8192]{2,1,0:T(8,128)(2,1)}, u32[]{:S(2)}) copy-start(bf16[1,64,8192]{2,1,0:T(8,128)(2,1)} %param.4) | copy-start | bytes 3145732
  2.7 23.9 %all-to-all-start = ((bf16[16,4,4096]{2,1,0:T(4,128)(2,1)}), bf16[16,4,4096]{2,1,0:T(4,128)(2,1)S(1)}, u32[]{:S(2)}, u32[]{:S(2)}) async-start(bf16[16,4,4096]{2,1,0:T(4,128)(2,1)} %bitcast.11), calls=%async_computation | async-start | bytes 1048576 | tf_op jit(solution)/shard_map/all_to_all | solution.py:19
  27.6 36.0 %all-to-all-start.2 = ((bf16[16,4,5120]{2,1,0:T(4,128)(2,1)}), bf16[16,4,5120]{2,1,0:T(4,128)(2,1)S(1)}, u32[]{:S(2)}, u32[]{:S(2)}) async-start(bf16[16,4,5120]{2,1,0:T(4,128)(2,1)} %reshape.39), calls=%async_computation.2 | async-start | bytes 1310720 | tf_op jit(solution)/shard_map/all_to_all | solution.py:19
  33.4 22.8 %collective-permute-start = (bf16[64,2048]{1,0:T(8,128)(2,1)S(1)}, bf16[64,2048]{1,0:T(8,128)(2,1)}, u32[]{:S(2)}, u32[]{:S(2)}) collective-permute-start(bf16[64,2048]{1,0:T(8,128)(2,1)S(1)} %get-tuple-element.6), channel_id=1, source_target_pairs={{0,8},{8,0},{64,72},{72,64},{1,9},{9,1},{65,73},{73,65},{2,10},{10... | collective-permute-start | bytes 786440 | tf_op jit(solution)/shard_map/ppermute | solution.py:62
  36.8 22.8 %collective-permute-start.1 = (bf16[64,2048]{1,0:T(8,128)(2,1)S(1)}, bf16[64,2048]{1,0:T(8,128)(2,1)}, u32[]{:S(2)}, u32[]{:S(2)}) collective-permute-start(bf16[64,2048]{1,0:T(8,128)(2,1)S(1)} %get-tuple-element.8), channel_id=1, source_target_pairs={{0,64},{8,72},{64,0},{72,8},{1,65},{9,73},{65,1},{73,9},{2,66},{10... | collective-permute-start | bytes 786440 | tf_op jit(solution)/shard_map/ppermute | solution.py:62
  40.1 23.6 %collective-permute-start.2 = (bf16[64,2048]{1,0:T(8,128)(2,1)S(1)}, bf16[64,2048]{1,0:T(8,128)(2,1)}, u32[]{:S(2)}, u32[]{:S(2)}) collective-permute-start(bf16[64,2048]{1,0:T(8,128)(2,1)S(1)} %get-tuple-element.7), channel_id=1, source_target_pairs={{0,72},{8,64},{64,8},{72,0},{1,73},{9,65},{65,9},{73,1},{2,74},{10... | collective-permute-start | bytes 786440 | tf_op jit(solution)/shard_map/ppermute | solution.py:62
  42.8 22.9 %collective-permute-start.3 = (bf16[64,2048]{1,0:T(8,128)(2,1)S(1)}, bf16[64,2048]{1,0:T(8,128)(2,1)}, u32[]{:S(2)}, u32[]{:S(2)}) collective-permute-start(bf16[64,2048]{1,0:T(8,128)(2,1)S(1)} %get-tuple-element.10), channel_id=1, source_target_pairs={{0,128},{128,256},{256,384},{384,0},{1,129},{129,257},{257,385},{3... | collective-permute-start | bytes 786440 | tf_op jit(solution)/shard_map/ppermute | solution.py:36
  45.2 24.5 %collective-permute-start.4 = (bf16[64,2048]{1,0:T(8,128)(2,1)S(1)}, bf16[64,2048]{1,0:T(8,128)(2,1)S(1)}, u32[]{:S(2)}, u32[]{:S(2)}) collective-permute-start(bf16[64,2048]{1,0:T(8,128)(2,1)S(1)} %get-tuple-element.10), channel_id=1, source_target_pairs={{0,384},{128,0},{256,128},{384,256},{1,385},{129,1},{257,129},{385... | collective-permute-start | bytes 786440 | tf_op jit(solution)/shard_map/ppermute | solution.py:36
  56.2 17.4 %collective-permute-start.5 = (bf16[64,2048]{1,0:T(8,128)(2,1)S(1)}, bf16[64,2048]{1,0:T(8,128)(2,1)}, u32[]{:S(2)}, u32[]{:S(2)}) collective-permute-start(bf16[64,2048]{1,0:T(8,128)(2,1)S(1)} %get-tuple-element.10), channel_id=1, source_target_pairs={{0,256},{128,384},{256,0},{384,128},{1,257},{129,385},{257,1},{385... | collective-permute-start | bytes 786440 | tf_op jit(solution)/shard_map/ppermute | solution.py:36
  59.5 18.5 %collective-permute-start.6 = (bf16[64,2048]{1,0:T(8,128)(2,1)S(1)}, bf16[64,2048]{1,0:T(8,128)(2,1)S(1)}, u32[]{:S(2)}, u32[]{:S(2)}) collective-permute-start(bf16[64,2048]{1,0:T(8,128)(2,1)S(1)} %get-tuple-element.9), channel_id=1, source_target_pairs={{0,128},{128,256},{256,384},{384,0},{1,129},{129,257},{257,385},{3... | collective-permute-start | bytes 786440 | tf_op jit(solution)/shard_map/ppermute | solution.py:36
  63.8 30.6 %collective-permute-start.7 = (bf16[64,2048]{1,0:T(8,128)(2,1)S(1)}, bf16[64,2048]{1,0:T(8,128)(2,1)S(1)}, u32[]{:S(2)}, u32[]{:S(2)}) collective-permute-start(bf16[64,2048]{1,0:T(8,128)(2,1)S(1)} %get-tuple-element.9), channel_id=1, source_target_pairs={{0,384},{128,0},{256,128},{384,256},{1,385},{129,1},{257,129},{385... | collective-permute-start | bytes 786440 | tf_op jit(solution)/shard_map/ppermute | solution.py:36
  65.7 28.7 %collective-permute-start.8 = (bf16[64,2048]{1,0:T(8,128)(2,1)S(1)}, bf16[64,2048]{1,0:T(8,128)(2,1)}, u32[]{:S(2)}, u32[]{:S(2)}) collective-permute-start(bf16[64,2048]{1,0:T(8,128)(2,1)S(1)} %get-tuple-element.9), channel_id=1, source_target_pairs={{0,256},{128,384},{256,0},{384,128},{1,257},{129,385},{257,1},{385... | collective-permute-start | bytes 786440 | tf_op jit(solution)/shard_map/ppermute | solution.py:36
  69.7 6.5 %copy-start.2 = (bf16[64,2048]{1,0:T(8,128)(2,1)}, bf16[64,2048]{1,0:T(8,128)(2,1)S(1)}, u32[]{:S(2)}) copy-start(bf16[64,2048]{1,0:T(8,128)(2,1)S(1)} %collective-permute-done.4) | copy-start | bytes 786436
  69.7 48.9 %collective-permute-start.10 = (bf16[64,5120]{1,0:T(8,128)(2,1)S(1)}, bf16[64,5120]{1,0:T(8,128)(2,1)S(1)}, u32[]{:S(2)}, u32[]{:S(2)}) collective-permute-start(bf16[64,5120]{1,0:T(8,128)(2,1)S(1)} %reshape.40), channel_id=1, source_target_pairs={{0,384},{128,0},{256,128},{384,256},{1,385},{129,1},{257,129},{385... | collective-permute-start | bytes 1966088 | tf_op jit(solution)/shard_map/ppermute | solution.py:36
  73.6 45.0 %collective-permute-start.11 = (bf16[64,5120]{1,0:T(8,128)(2,1)S(1)}, bf16[64,5120]{1,0:T(8,128)(2,1)}, u32[]{:S(2)}, u32[]{:S(2)}) collective-permute-start(bf16[64,5120]{1,0:T(8,128)(2,1)S(1)} %reshape.40), channel_id=1, source_target_pairs={{0,256},{128,384},{256,0},{384,128},{1,257},{129,385},{257,1},{385... | collective-permute-start | bytes 1966088 | tf_op jit(solution)/shard_map/ppermute | solution.py:36
  78.0 40.6 %collective-permute-start.9 = (bf16[64,5120]{1,0:T(8,128)(2,1)S(1)}, bf16[64,5120]{1,0:T(8,128)(2,1)}, u32[]{:S(2)}, u32[]{:S(2)}) collective-permute-start(bf16[64,5120]{1,0:T(8,128)(2,1)S(1)} %reshape.40), channel_id=1, source_target_pairs={{0,128},{128,256},{256,384},{384,0},{1,129},{129,257},{257,385},{3... | collective-permute-start | bytes 1966088 | tf_op jit(solution)/shard_map/ppermute | solution.py:36
  82.8 17.5 %all-to-all-start.1 = ((f32[4,64,256]{2,1,0:T(8,128)}), f32[4,64,256]{2,1,0:T(8,128)S(1)}, u32[]{:S(2)}, u32[]{:S(2)}) async-start(f32[4,64,256]{2,1,0:T(8,128)} %bitcast.12), calls=%async_computation.1 | async-start | bytes 524288 | tf_op jit(solution)/shard_map/all_to_all | solution.py:19
  94.4 0.7 copy-start.3

commit v3 on v2

--- a/solution.py
+++ b/solution.py
@@ -3,10 +3,11 @@
 import jax
 import jax.numpy as jnp
 from jax import lax
+from jax.experimental import pallas as pl
 from jax.sharding import Mesh, PartitionSpec as P
 
 
-CUTS = (0, 4, 14)
+CUTS = (0, 7, 28)
 
 
 def gram_of(left, right):
@@ -28,10 +29,34 @@
     return rows.reshape(-1, shape[1])
 
 
+def first_blocks(val_a, val_g, part, cols):
+    tokens = val_a.shape[0]
+    half = lax.axis_size("yh")
+    peers = [(z, h, p) for z in range(2) for h in range(half) for p in range(2)]
+
+    def body(a, g, out):
+        for i, (z, _, p) in enumerate(peers):
+            q = 2 * z + p
+            out[i, :, :part] = a[:, q * part : (q + 1) * part]
+            out[i, :, part:] = g[...]
+
+    return pl.pallas_call(
+        body,
+        grid=(1,),
+        in_specs=[
+            pl.BlockSpec(val_a.shape, lambda i: (0, 0)),
+            pl.BlockSpec((tokens, cols), lambda i: (0, 0)),
+        ],
+        out_specs=pl.BlockSpec((len(peers), tokens, part + cols), lambda i: (0, 0, 0)),
+        out_shape=jax.ShapeDtypeStruct((len(peers), tokens, part + cols), val_a.dtype),
+        name="first_blocks",
+    )(val_a, val_g)
+
+
 def across(rows):
     n = lax.axis_size("x")
     moved = []
-    for by in (1, -1, 2):
+    for by in (2, 1, -1):
         pairs = [(j, (j + by) % n) for j in range(n)]
         moved.append(lax.ppermute(rows, "x", pairs))
     return jnp.concatenate([rows, *moved])
@@ -50,10 +75,9 @@
     unit = grad.shape[1] // CUTS[-1]
     spans = [(unit * a, unit * b) for a, b in zip(CUTS, CUTS[1:])]
 
-    first = val_g[:, : spans[0][1]]
-    quarters = [val_a[:, q * part : (q + 1) * part] for q in range(size)]
-    blocks = jnp.stack([jnp.concatenate([q, first], axis=1) for q in quarters])
-    planes = [plane(blocks.reshape((2, 2) + blocks.shape[1:]))]
+    blocks = first_blocks(val_a, val_g, part, spans[0][1])
+    rows_of = exchange(blocks, ("zl", "yh", "yl"))
+    planes = [rows_of.reshape(-1, blocks.shape[2])]
 
     pieces = []
     for j in range(size):
@@ -76,12 +100,15 @@
     )
     act_gram = exchange(act_gram.reshape(size, rows, -1), team)
     act_gram = jnp.sum(act_gram, axis=0)
-    act_gram = lax.all_gather(act_gram, "t", axis=0, tiled=True)
+    act_gram = jnp.broadcast_to(act_gram[None], (groups,) + act_gram.shape)
+    act_gram = exchange(act_gram, "t")
+    act_gram = act_gram.reshape(-1, act_gram.shape[-1])
 
     grad_gram = 0.0
     for i, (a, b) in enumerate(spans):
         grad_gram = lax.optimization_barrier(grad_gram)
-        grad_gram = grad_gram + gram_of(grad[:, a:b], across(planes[i]))
+        vals = across(planes[i])
+        grad_gram = grad_gram + gram_of(grad[:, a:b], vals)
     folded = jnp.sum(act_gram * grad_gram, axis=1) * factor
     folded = exchange(folded.reshape(groups * layers, -1), ("t", "s"))
     return jnp.sum(folded, axis=0)

time: 136 us -> 138 us (1.015)
  the two profiles are of different devices: /device:TPU:22 before, /device:TPU:1 now
where the time goes in v3:
time: 138 us; the launch traced here: 137 us
  starting transfers between devices  68.2 us (49%)
  waiting for transfers between devices  36.8 us (27%)
  blocking collectives  19.4 us (14%)
  matrix products  6.02 us (4%)
  local copies, waits for them, and re-layouts  3.23 us (2%)
  Pallas kernels  1.75 us (1%)
    ppermute x9, starting transfers between devices, across(): moved.append(lax.ppermute(rows, 'x', pairs))  31.2 us
    all_to_all x4, starting transfers between devices, exchange(): return lax.all_to_all(blocks, axes, split_axis=0, concat_axis=0, tiled=True)  28.6 us
    all_to_all x1, blocking collectives, exchange(): return lax.all_to_all(blocks, axes, split_axis=0, concat_axis=0, tiled=True)  19.4 us
    ppermute x9, waiting for transfers between devices, across(): moved.append(lax.ppermute(rows, 'x', pairs))  16.2 us
    all_to_all x4, waiting for transfers between devices, exchange(): return lax.all_to_all(blocks, axes, split_axis=0, concat_axis=0, tiled=True)  11.9 us
    ppermute x3, waiting for transfers between devices, local(): piece = lax.ppermute(piece, team, [(i, i ^ j) for i in range(size)])  8.7 us
    ppermute x3, starting transfers between devices, local(): piece = lax.ppermute(piece, team, [(i, i ^ j) for i in range(size)])  8.37 us
    dot_general x3, matrix products, gram_of(): lax.dot_general(left, right, (((1,), (1,)), ((), ())), preferred_element_...  6.02 us
  transfers between devices with their start and end apart: 16, of which 5 were waited for; matrix products, arithmetic and copies ran while one was open for 4% of the time, Pallas kernels for 0%

profile of v3, /device:TPU:1, one launch (start us, length us, event | category | flops | bytes accessed | tf_op | source)
XLA Modules:
  0.0 137.0 jit_solution(5276441802064350450)
XLA Ops:
  0.0 0.0 copy-start
  0.0 1.8 %first_blocks.1 = bf16[16,4,3840]{2,1,0:T(4,128)(2,1)} custom-call(bf16[4,8192]{1,0:T(4,128)(2,1)} %bitcast.21, bf16[4,7168]{1,0:T(4,128)(2,1)} %bitcast.19), custom_call_target="tpu_custom_call" | custom-call | tf_op jit(solution)/shard_map/first_blocks/pallas_call | solution.py:43
  1.8 9.6 %all-to-all-start = ((bf16[16,4,3840]{2,1,0:T(4,128)(2,1)}), bf16[16,4,3840]{2,1,0:T(4,128)(2,1)S(1)}, u32[]{:S(2)}, u32[]{:S(2)}) async-start(bf16[16,4,3840]{2,1,0:T(4,128)(2,1)} %first_blocks.1), calls=%async_computation | async-start | bytes 983040 | tf_op jit(solution)/shard_map/all_to_all | solution.py:20
  11.3 0.8 slice.23
  12.1 11.9 %all-to-all-done = bf16[16,4,3840]{2,1,0:T(4,128)(2,1)S(1)} async-done(((bf16[16,4,3840]{2,1,0:T(4,128)(2,1)}), bf16[16,4,3840]{2,1,0:T(4,128)(2,1)S(1)}, u32[]{:S(2)}, u32[]{:S(2)}) %all-to-all-start) | async-done | bytes 491552 | tf_op jit(solution)/shard_map/all_to_all | solution.py:20
  24.0 1.0 reshape.39
  25.0 6.5 %all-to-all-start.3 = ((bf16[16,4,5376]{2,1,0:T(4,128)(2,1)}), bf16[16,4,5376]{2,1,0:T(4,128)(2,1)S(1)}, u32[]{:S(2)}, u32[]{:S(2)}) async-start(bf16[16,4,5376]{2,1,0:T(4,128)(2,1)} %reshape.39), calls=%async_computation.3 | async-start | bytes 1376256 | tf_op jit(solution)/shard_map/all_to_all | solution.py:20
  31.6 0.0 copy-done
  31.6 0.1 dynamic-slice_bitcast_fusion.3
  31.7 3.2 %collective-permute-start = (bf16[64,2048]{1,0:T(8,128)(2,1)S(1)}, bf16[64,2048]{1,0:T(8,128)(2,1)S(1)}, u32[]{:S(2)}, u32[]{:S(2)}) collective-permute-start(bf16[64,2048]{1,0:T(8,128)(2,1)S(1)} %get-tuple-element.6), channel_id=1, source_target_pairs={{0,8},{8,0},{64,72},{72,64},{1,9},{9,1},{65,73},{73,65},{2,10},{10... | collective-permute-start | bytes 786440 | tf_op jit(solution)/shard_map/ppermute | solution.py:86
  35.0 3.1 %collective-permute-start.1 = (bf16[64,2048]{1,0:T(8,128)(2,1)S(1)}, bf16[64,2048]{1,0:T(8,128)(2,1)S(1)}, u32[]{:S(2)}, u32[]{:S(2)}) collective-permute-start(bf16[64,2048]{1,0:T(8,128)(2,1)S(1)} %get-tuple-element.8), channel_id=1, source_target_pairs={{0,64},{8,72},{64,0},{72,8},{1,65},{9,73},{65,1},{73,9},{2,66},{10... | collective-permute-start | bytes 786440 | tf_op jit(solution)/shard_map/ppermute | solution.py:86
  38.1 2.0 %collective-permute-start.2 = (bf16[64,2048]{1,0:T(8,128)(2,1)S(1)}, bf16[64,2048]{1,0:T(8,128)(2,1)S(1)}, u32[]{:S(2)}, u32[]{:S(2)}) collective-permute-start(bf16[64,2048]{1,0:T(8,128)(2,1)S(1)} %get-tuple-element.7), channel_id=1, source_target_pairs={{0,72},{8,64},{64,8},{72,0},{1,73},{9,65},{65,9},{73,1},{2,74},{10... | collective-permute-start | bytes 786440 | tf_op jit(solution)/shard_map/ppermute | solution.py:86
  40.1 0.1 reshape.36
  40.2 4.7 %collective-permute-start.3 = (bf16[64,2048]{1,0:T(8,128)(2,1)S(1)}, bf16[64,2048]{1,0:T(8,128)(2,1)}, u32[]{:S(2)}, u32[]{:S(2)}) collective-permute-start(bf16[64,2048]{1,0:T(8,128)(2,1)S(1)} %slice.20), channel_id=1, source_target_pairs={{0,256},{128,384},{256,0},{384,128},{1,257},{129,385},{257,1},{385... | collective-permute-start | bytes 786440 | tf_op jit(solution)/shard_map/ppermute | solution.py:61
  44.9 2.2 %collective-permute-start.4 = (bf16[64,2048]{1,0:T(8,128)(2,1)S(1)}, bf16[64,2048]{1,0:T(8,128)(2,1)}, u32[]{:S(2)}, u32[]{:S(2)}) collective-permute-start(bf16[64,2048]{1,0:T(8,128)(2,1)S(1)} %slice.20), channel_id=1, source_target_pairs={{0,128},{128,256},{256,384},{384,0},{1,129},{129,257},{257,385},{3... | collective-permute-start | bytes 786440 | tf_op jit(solution)/shard_map/ppermute | solution.py:61
  47.1 6.7 %collective-permute-done = bf16[64,2048]{1,0:T(8,128)(2,1)S(1)} collective-permute-done((bf16[64,2048]{1,0:T(8,128)(2,1)S(1)}, bf16[64,2048]{1,0:T(8,128)(2,1)S(1)}, u32[]{:S(2)}, u32[]{:S(2)}) %collective-permute-start) | collective-permute-done | bytes 262176 | tf_op jit(solution)/shard_map/ppermute | solution.py:86
  53.8 4.4 %collective-permute-start.5 = (bf16[64,2048]{1,0:T(8,128)(2,1)S(1)}, bf16[64,2048]{1,0:T(8,128)(2,1)S(1)}, u32[]{:S(2)}, u32[]{:S(2)}) collective-permute-start(bf16[64,2048]{1,0:T(8,128)(2,1)S(1)} %slice.20), channel_id=1, source_target_pairs={{0,384},{128,0},{256,128},{384,256},{1,385},{129,1},{257,129},{385... | collective-permute-start | bytes 786440 | tf_op jit(solution)/shard_map/ppermute | solution.py:61
  58.2 0.0 collective-permute-done.1
  58.2 2.0 %collective-permute-done.2 = bf16[64,2048]{1,0:T(8,128)(2,1)S(1)} collective-permute-done((bf16[64,2048]{1,0:T(8,128)(2,1)S(1)}, bf16[64,2048]{1,0:T(8,128)(2,1)S(1)}, u32[]{:S(2)}, u32[]{:S(2)}) %collective-permute-start.2) | collective-permute-done | bytes 262176 | tf_op jit(solution)/shard_map/ppermute | solution.py:86
  60.2 0.0 collective-permute-done.3
  60.2 0.0 collective-permute-done.4
  60.3 1.3 collective-permute-done.5
  61.5 1.5 %fusion.15 = f32[256,256]{1,0:T(8,128)S(1)} fusion(bf16[64,2048]{1,0:T(8,128)(2,1)S(1)} %collective-permute-done.2, bf16[64,2048]{1,0:T(8,128)(2,1)S(1)} %collective-permute-done.1, bf16[64,2048]{1,0:T(8,128)(2,1)S(1)} %collective-permute-done, bf16[64,2048]{1,0:T(8,128)(2,1)S(1)} %get-tuple-element.5, bf16[64,2048]{1,0:T(8,128)(2,1)S(1)} %collective-permute-done.5, ...), kind=kOutput, calls=%fused_computation.12 | convolution fusion | flops 276824064 | bytes 2359296 | tf_op jit(solution)/shard_map/dot_general | solution.py:14
  63.1 0.7 pad_maximum_fusion
  63.8 0.0 all-to-all-done.3
  63.8 3.4 %all-to-all-start.1 = ((f32[4,64,256]{2,1,0:T(8,128)}), f32[4,64,256]{2,1,0:T(8,128)S(1)}, u32[]{:S(2)}, u32[]{:S(2)}) async-start(f32[4,64,256]{2,1,0:T(8,128)} %bitcast.6), calls=%async_computation.1 | async-start | bytes 524288 | tf_op jit(solution)/shard_map/all_to_all | solution.py:20
  67.2 4.4 %collective-permute-start.6 = (bf16[64,1792]{1,0:T(8,128)(2,1)S(1)}, bf16[64,1792]{1,0:T(8,128)(2,1)S(1)}, u32[]{:S(2)}, u32[]{:S(2)}) collective-permute-start(bf16[64,1792]{1,0:T(8,128)(2,1)S(1)} %slice.21), channel_id=1, source_target_pairs={{0,256},{128,384},{256,0},{384,128},{1,257},{129,385},{257,1},{385... | collective-permute-start | bytes 688136 | tf_op jit(solution)/shard_map/ppermute | solution.py:61
  71.7 0.2 reshape.40
  71.8 3.4 %collective-permute-start.10 = (bf16[64,5376]{1,0:T(8,128)(2,1)S(1)}, bf16[64,5376]{1,0:T(8,128)(2,1)S(1)}, u32[]{:S(2)}, u32[]{:S(2)}) collective-permute-start(bf16[64,5376]{1,0:T(8,128)(2,1)S(1)} %reshape.40), channel_id=1, source_target_pairs={{0,128},{128,256},{256,384},{384,0},{1,129},{129,257},{257,385},{3... | collective-permute-start | bytes 2064392 | tf_op jit(solution)/shard_map/ppermute | solution.py:61
  75.3 3.1 %collective-permute-start.11 = (bf16[64,5376]{1,0:T(8,128)(2,1)S(1)}, bf16[64,5376]{1,0:T(8,128)(2,1)S(1)}, u32[]{:S(2)}, u32[]{:S(2)}) collective-permute-start(bf16[64,5376]{1,0:T(8,128)(2,1)S(1)} %reshape.40), channel_id=1, source_target_pairs={{0,384},{128,0},{256,128},{384,256},{1,385},{129,1},{257,129},{385... | collective-permute-start | bytes 2064392 | tf_op jit(solution)/shard_map/ppermute | solution.py:61
  78.3 2.6 %collective-permute-start.9 = (bf16[64,5376]{1,0:T(8,128)(2,1)S(1)}, bf16[64,5376]{1,0:T(8,128)(2,1)}, u32[]{:S(2)}, u32[]{:S(2)}) collective-permute-start(bf16[64,5376]{1,0:T(8,128)(2,1)S(1)} %reshape.40), channel_id=1, source_target_pairs={{0,256},{128,384},{256,0},{384,128},{1,257},{129,385},{257,1},{385... | collective-permute-start | bytes 2064392 | tf_op jit(solution)/shard_map/ppermute | solution.py:61
  80.9 1.9 %collective-permute-start.7 = (bf16[64,1792]{1,0:T(8,128)(2,1)S(1)}, bf16[64,1792]{1,0:T(8,128)(2,1)S(1)}, u32[]{:S(2)}, u32[]{:S(2)}) collective-permute-start(bf16[64,1792]{1,0:T(8,128)(2,1)S(1)} %slice.21), channel_id=1, source_target_pairs={{0,128},{128,256},{256,384},{384,0},{1,129},{129,257},{257,385},{3... | collective-permute-start | bytes 688136 | tf_op jit(solution)/shard_map/ppermute | solution.py:61
  82.8 0.0 collective-permute-done.6
  82.8 4.6 %collective-permute-start.8 = (bf16[64,1792]{1,0:T(8,128)(2,1)S(1)}, bf16[64,1792]{1,0:T(8,128)(2,1)S(1)}, u32[]{:S(2)}, u32[]{:S(2)}) collective-permute-start(bf16[64,1792]{1,0:T(8,128)(2,1)S(1)} %slice.21), channel_id=1, source_target_pairs={{0,384},{128,0},{256,128},{384,256},{1,385},{129,1},{257,129},{385... | collective-permute-start | bytes 688136 | tf_op jit(solution)/shard_map/ppermute | solution.py:61
  87.4 0.0 all-to-all-done.1
  87.4 0.7 broadcast_in_dim.2
  88.2 9.1 %all-to-all-start.2 = ((f32[4,64,256]{2,1,0:T(8,128)}), f32[4,64,256]{2,1,0:T(8,128)S(1)}, u32[]{:S(2)}, u32[]{:S(2)}) async-start(f32[4,64,256]{2,1,0:T(8,128)} %broadcast_in_dim.2), calls=%async_computation.2 | async-start | bytes 524288 | tf_op jit(solution)/shard_map/all_to_all | solution.py:20
  97.3 14.9 %collective-permute-done.7 = bf16[64,1792]{1,0:T(8,128)(2,1)S(1)} collective-permute-done((bf16[64,1792]{1,0:T(8,128)(2,1)S(1)}, bf16[64,1792]{1,0:T(8,128)(2,1)S(1)}, u32[]{:S(2)}, u32[]{:S(2)}) %collective-permute-start.7) | collective-permute-done | bytes 229408 | tf_op jit(solution)/shard_map/ppermute | solution.py:61
  112.2 0.0 collective-permute-done.8
  112.2 1.6 %fusion.14 = f32[256,256]{0,1:T(8,128)S(1)} fusion(bf16[256,7168]{1,0:T(8,128)(2,1)} %bitcast.23, bf16[64,1792]{1,0:T(8,128)(2,1)S(1)} %collective-permute-done.8, bf16[64,1792]{1,0:T(8,128)(2,1)S(1)} %collective-permute-done.7, bf16[64,1792]{1,0:T(8,128)(2,1)S(1)} %collective-permute-done.6, bf16[64,1792]{1,0:T(8,128)(2,1)S(1)} %slice.21, f32[]{:T(128)} %constant.32.clone.1), kind=kOutput, calls=%fused_computation.11 | convolution fusion | flops 238616576 | bytes 2097664 | tf_op jit(solution)/shard_map/dot_general | solution.py:14
  113.8 0.0 all-to-all-done.2
  113.8 0.1 copy.7
  114.0 0.0 collective-permute-done.10
  114.0 0.0 collective-permute-done.11
  114.0 0.0 collective-permute-done.9
  114.0 2.9 %fusion.9 = f32[256,256]{0,1:T(8,128)S(1)} fusion(bf16[256,7168]{1,0:T(8,128)(2,1)} %bitcast.24, bf16[64,5376]{1,0:T(8,128)(2,1)S(1)} %collective-permute-done.11, bf16[64,5376]{1,0:T(8,128)(2,1)S(1)} %collective-permute-done.10, bf16[64,5376]{1,0:T(8,128)(2,1)} %collective-permute-done.9, bf16[64,5376]{1,0:T(8,128)(2,1)S(1)} %reshape.40), kind=kOutput, calls=%fused_computation.9 | convolution fusion | flops 715653120 | bytes 5767168 | tf_op jit(solution)/shard_map/dot_general | solution.py:14
  116.9 0.1 multiply_reduce_fusion
  117.0 0.1 mul.59
  117.1 19.4 %all_to_all.26 = f32[8,1,32]{2,1,0:T(1,128)S(1)} all-to-all(f32[8,1,32]{2,1,0:T(1,128)S(1)} %mul.59), channel_id=1, replica_groups=mesh['x'=4,'zl'=2,'yh'=4,'yl'=2,'t'=4,'s'=2] {'t','s'}, dimensions={0} | all-to-all | bytes 2048 | tf_op jit(solution)/shard_map/all_to_all | solution.py:20
  136.4 0.5 reduce_sum.29
  (5 shorter events, 0.1 us)
Async XLA Ops:
  0.0 31.6 %copy-start = (bf16[1,64,8192]{2,1,0:T(8,128)(2,1)S(1)}, bf16[1,64,8192]{2,1,0:T(8,128)(2,1)}, u32[]{:S(2)}) copy-start(bf16[1,64,8192]{2,1,0:T(8,128)(2,1)} %param.4) | copy-start | bytes 3145732
  1.8 22.2 %all-to-all-start = ((bf16[16,4,3840]{2,1,0:T(4,128)(2,1)}), bf16[16,4,3840]{2,1,0:T(4,128)(2,1)S(1)}, u32[]{:S(2)}, u32[]{:S(2)}) async-start(bf16[16,4,3840]{2,1,0:T(4,128)(2,1)} %first_blocks.1), calls=%async_computation | async-start | bytes 983040 | tf_op jit(solution)/shard_map/all_to_all | solution.py:20
  25.0 38.8 %all-to-all-start.3 = ((bf16[16,4,5376]{2,1,0:T(4,128)(2,1)}), bf16[16,4,5376]{2,1,0:T(4,128)(2,1)S(1)}, u32[]{:S(2)}, u32[]{:S(2)}) async-start(bf16[16,4,5376]{2,1,0:T(4,128)(2,1)} %reshape.39), calls=%async_computation.3 | async-start | bytes 1376256 | tf_op jit(solution)/shard_map/all_to_all | solution.py:20
  31.7 22.1 %collective-permute-start = (bf16[64,2048]{1,0:T(8,128)(2,1)S(1)}, bf16[64,2048]{1,0:T(8,128)(2,1)S(1)}, u32[]{:S(2)}, u32[]{:S(2)}) collective-permute-start(bf16[64,2048]{1,0:T(8,128)(2,1)S(1)} %get-tuple-element.6), channel_id=1, source_target_pairs={{0,8},{8,0},{64,72},{72,64},{1,9},{9,1},{65,73},{73,65},{2,10},{10... | collective-permute-start | bytes 786440 | tf_op jit(solution)/shard_map/ppermute | solution.py:86
  35.0 23.3 %collective-permute-start.1 = (bf16[64,2048]{1,0:T(8,128)(2,1)S(1)}, bf16[64,2048]{1,0:T(8,128)(2,1)S(1)}, u32[]{:S(2)}, u32[]{:S(2)}) collective-permute-start(bf16[64,2048]{1,0:T(8,128)(2,1)S(1)} %get-tuple-element.8), channel_id=1, source_target_pairs={{0,64},{8,72},{64,0},{72,8},{1,65},{9,73},{65,1},{73,9},{2,66},{10... | collective-permute-start | bytes 786440 | tf_op jit(solution)/shard_map/ppermute | solution.py:86
  38.1 22.2 %collective-permute-start.2 = (bf16[64,2048]{1,0:T(8,128)(2,1)S(1)}, bf16[64,2048]{1,0:T(8,128)(2,1)S(1)}, u32[]{:S(2)}, u32[]{:S(2)}) collective-permute-start(bf16[64,2048]{1,0:T(8,128)(2,1)S(1)} %get-tuple-element.7), channel_id=1, source_target_pairs={{0,72},{8,64},{64,8},{72,0},{1,73},{9,65},{65,9},{73,1},{2,74},{10... | collective-permute-start | bytes 786440 | tf_op jit(solution)/shard_map/ppermute | solution.py:86
  40.2 20.0 %collective-permute-start.3 = (bf16[64,2048]{1,0:T(8,128)(2,1)S(1)}, bf16[64,2048]{1,0:T(8,128)(2,1)}, u32[]{:S(2)}, u32[]{:S(2)}) collective-permute-start(bf16[64,2048]{1,0:T(8,128)(2,1)S(1)} %slice.20), channel_id=1, source_target_pairs={{0,256},{128,384},{256,0},{384,128},{1,257},{129,385},{257,1},{385... | collective-permute-start | bytes 786440 | tf_op jit(solution)/shard_map/ppermute | solution.py:61
  44.9 15.3 %collective-permute-start.4 = (bf16[64,2048]{1,0:T(8,128)(2,1)S(1)}, bf16[64,2048]{1,0:T(8,128)(2,1)}, u32[]{:S(2)}, u32[]{:S(2)}) collective-permute-start(bf16[64,2048]{1,0:T(8,128)(2,1)S(1)} %slice.20), channel_id=1, source_target_pairs={{0,128},{128,256},{256,384},{384,0},{1,129},{129,257},{257,385},{3... | collective-permute-start | bytes 786440 | tf_op jit(solution)/shard_map/ppermute | solution.py:61
  53.8 7.7 %collective-permute-start.5 = (bf16[64,2048]{1,0:T(8,128)(2,1)S(1)}, bf16[64,2048]{1,0:T(8,128)(2,1)S(1)}, u32[]{:S(2)}, u32[]{:S(2)}) collective-permute-start(bf16[64,2048]{1,0:T(8,128)(2,1)S(1)} %slice.20), channel_id=1, source_target_pairs={{0,384},{128,0},{256,128},{384,256},{1,385},{129,1},{257,129},{385... | collective-permute-start | bytes 786440 | tf_op jit(solution)/shard_map/ppermute | solution.py:61
  63.8 23.6 %all-to-all-start.1 = ((f32[4,64,256]{2,1,0:T(8,128)}), f32[4,64,256]{2,1,0:T(8,128)S(1)}, u32[]{:S(2)}, u32[]{:S(2)}) async-start(f32[4,64,256]{2,1,0:T(8,128)} %bitcast.6), calls=%async_computation.1 | async-start | bytes 524288 | tf_op jit(solution)/shard_map/all_to_all | solution.py:20
  67.2 15.6 %collective-permute-start.6 = (bf16[64,1792]{1,0:T(8,128)(2,1)S(1)}, bf16[64,1792]{1,0:T(8,128)(2,1)S(1)}, u32[]{:S(2)}, u32[]{:S(2)}) collective-permute-start(bf16[64,1792]{1,0:T(8,128)(2,1)S(1)} %slice.21), channel_id=1, source_target_pairs={{0,256},{128,384},{256,0},{384,128},{1,257},{129,385},{257,1},{385... | collective-permute-start | bytes 688136 | tf_op jit(solution)/shard_map/ppermute | solution.py:61
  71.8 42.2 %collective-permute-start.10 = (bf16[64,5376]{1,0:T(8,128)(2,1)S(1)}, bf16[64,5376]{1,0:T(8,128)(2,1)S(1)}, u32[]{:S(2)}, u32[]{:S(2)}) collective-permute-start(bf16[64,5376]{1,0:T(8,128)(2,1)S(1)} %reshape.40), channel_id=1, source_target_pairs={{0,128},{128,256},{256,384},{384,0},{1,129},{129,257},{257,385},{3... | collective-permute-start | bytes 2064392 | tf_op jit(solution)/shard_map/ppermute | solution.py:61
  75.3 38.7 %collective-permute-start.11 = (bf16[64,5376]{1,0:T(8,128)(2,1)S(1)}, bf16[64,5376]{1,0:T(8,128)(2,1)S(1)}, u32[]{:S(2)}, u32[]{:S(2)}) collective-permute-start(bf16[64,5376]{1,0:T(8,128)(2,1)S(1)} %reshape.40), channel_id=1, source_target_pairs={{0,384},{128,0},{256,128},{384,256},{1,385},{129,1},{257,129},{385... | collective-permute-start | bytes 2064392 | tf_op jit(solution)/shard_map/ppermute | solution.py:61
  78.3 35.7 %collective-permute-start.9 = (bf16[64,5376]{1,0:T(8,128)(2,1)S(1)}, bf16[64,5376]{1,0:T(8,128)(2,1)}, u32[]{:S(2)}, u32[]{:S(2)}) collective-permute-start(bf16[64,5376]{1,0:T(8,128)(2,1)S(1)} %reshape.40), channel_id=1, source_target_pairs={{0,256},{128,384},{256,0},{384,128},{1,257},{129,385},{257,1},{385... | collective-permute-start | bytes 2064392 | tf_op jit(solution)/shard_map/ppermute | solution.py:61
  80.9 31.3 %collective-permute-start.7 = (bf16[64,1792]{1,0:T(8,128)(2,1)S(1)}, bf16[64,1792]{1,0:T(8,128)(2,1)S(1)}, u32[]{:S(2)}, u32[]{:S(2)}) collective-permute-start(bf16[64,1792]{1,0:T(8,128)(2,1)S(1)} %slice.21), channel_id=1, source_target_pairs={{0,128},{128,256},{256,384},{384,0},{1,129},{129,257},{257,385},{3... | collective-permute-start | bytes 688136 | tf_op jit(solution)/shard_map/ppermute | solution.py:61
  82.8 29.4 %collective-permute-start.8 = (bf16[64,1792]{1,0:T(8,128)(2,1)S(1)}, bf16[64,1792]{1,0:T(8,128)(2,1)S(1)}, u32[]{:S(2)}, u32[]{:S(2)}) collective-permute-start(bf16[64,1792]{1,0:T(8,128)(2,1)S(1)} %slice.21), channel_id=1, source_target_pairs={{0,384},{128,0},{256,128},{384,256},{1,385},{129,1},{257,129},{385... | collective-permute-start | bytes 688136 | tf_op jit(solution)/shard_map/ppermute | solution.py:61
  88.2 25.7 %all-to-all-start.2 = ((f32[4,64,256]{2,1,0:T(8,128)}), f32[4,64,256]{2,1,0:T(8,128)S(1)}, u32[]{:S(2)}, u32[]{:S(2)}) async-start(f32[4,64,256]{2,1,0:T(8,128)} %broadcast_in_dim.2), calls=%async_computation.2 | async-start | bytes 524288 | tf_op jit(solution)/shard_map/all_to_all | solution.py:20
